TPU v7x, 32 devices: a whole 2x2x4 slice. The times are simulated.
32 devices in a mesh: dp: 4 (over y, x), tensor: 8 (over z, core).
Axes of the slice: x: 2, y: 2, z: 4, core: 2. Of those that a mesh axis runs over, the one named last changes fastest.
Arguments:
- normed_input: bfloat16 [4096, 8192], P('dp', 'tensor'), may hold values from -6 to 6
- positions: int32 [4096], P('dp'), may hold values from 0 to 4095
- fixed_weight_matrix: bfloat16 [8192, 10240], P('dp', 'tensor'), may hold values from -0.09375 to 0.09375
- adapter_down_map: bfloat16 [8192, 16], P('tensor'), may hold values from -0.0625 to 0.0625
- adapter_up_map: bfloat16 [16, 10240], P(None, 'tensor'), may hold values from -0.0625 to 0.0625
- output_gradient: bfloat16 [4096, 10240], P('dp', 'tensor'), may hold values from -6 to 6
Outputs:
- grad_x: bfloat16 [4096, 8192], P('dp', 'tensor')
- grad_a: float32 [8192, 16], P('tensor')
- grad_b: float32 [16, 10240], P(None, 'tensor')
All inputs are finite; a program needn't handle non-finite values.
Results may differ from a plain program's by a relative error of at most 0.0048.
Values may be sent and summed in bfloat16 or wider, within the bound.
A program may use at most 256 MiB of HBM per device.

v0:
```python
import math

import jax
import jax.numpy as jnp
from jax import lax
from jax.sharding import PartitionSpec as P

MODEL_WIDTH = 8192
KV = 1024
HEAD = 128


def rope_tables(positions, width, shards, shard):
    q_width = MODEL_WIDTH // shards
    k_width = KV // shards
    offset = jnp.arange(width, dtype=jnp.int32)
    is_query = offset < q_width
    is_key = jnp.logical_and(offset >= q_width, offset < q_width + k_width)
    dimension = jnp.where(
        is_query, (shard * q_width + offset) % HEAD, (shard * k_width + offset - q_width) % HEAD
    )
    pair = (dimension // 2).astype(jnp.float32)
    freq = jnp.float32(500000.0) ** (-2.0 * pair / HEAD)
    angle = positions.astype(jnp.float32)[:, None] * freq[None, :]
    rotate = jnp.logical_or(is_query, is_key)[None, :]
    cosine = jnp.where(rotate, jnp.cos(angle), jnp.float32(1.0))
    sine = jnp.where(rotate, jnp.sin(angle), jnp.float32(0.0))
    return (cosine[:, 0::2], sine[:, 0::2])


def on_device(
    normed_input, positions, fixed_weight_matrix, adapter_down_map, adapter_up_map, output_gradient
):
    rows, width = output_gradient.shape
    shards = lax.axis_size("tensor")
    shard = lax.axis_index("tensor")
    cosine, sine = rope_tables(positions, width, shards, shard)
    pairs = output_gradient.astype(jnp.float32).reshape(rows, width // 2, 2)
    first = pairs[:, :, 0] * cosine + pairs[:, :, 1] * sine
    second = pairs[:, :, 1] * cosine - pairs[:, :, 0] * sine
    unrotated_gradient = (
        jnp.stack([first, second], axis=2).reshape(rows, width).astype(jnp.bfloat16)
    )
    rank_input = jnp.dot(normed_input, adapter_down_map, preferred_element_type=jnp.float32)
    rank_gradient = jnp.dot(
        unrotated_gradient, adapter_up_map.T, preferred_element_type=jnp.float32
    )
    rank_input, rank_gradient = lax.psum((rank_input, rank_gradient), "tensor")
    low_xb = rank_input.astype(jnp.bfloat16)
    rank_gradient_up = rank_gradient.astype(jnp.bfloat16)
    factor = 2.0 / math.sqrt(rows * lax.axis_size("dp"))
    part_a = factor * jnp.dot(normed_input.T, rank_gradient_up, preferred_element_type=jnp.float32)
    part_b = factor * jnp.dot(low_xb.T, unrotated_gradient, preferred_element_type=jnp.float32)
    terms = jnp.dot(
        unrotated_gradient,
        lax.all_gather(fixed_weight_matrix, "dp", axis=0, tiled=True).T,
        preferred_element_type=jnp.float32,
    )
    base = lax.psum_scatter(terms, "tensor", scatter_dimension=1, tiled=True)
    adapter_branch = jnp.dot(
        rank_gradient_up, adapter_down_map.T, preferred_element_type=jnp.float32
    )
    grad_x = (base + 2.0 * adapter_branch).astype(jnp.bfloat16)
    grad_a, grad_b = lax.psum((part_a, part_b), "dp")
    return (grad_x, grad_a, grad_b)


def solution(mesh):
    placed = (
        P("dp", "tensor"),
        P("dp"),
        P("dp", "tensor"),
        P("tensor", None),
        P(None, "tensor"),
        P("dp", "tensor"),
    )
    return jax.shard_map(
        on_device,
        mesh=mesh,
        in_specs=placed,
        out_specs=(P("dp", "tensor"), P("tensor", None), P(None, "tensor")),
        check_vma=False,
    )
```

profile of v0, /device:TPU:6, one launch (start us, length us, event | category | flops | bytes accessed | tf_op | source)
XLA Modules:
  0.0 623.1 jit_solution(5402647830640319153)
XLA Ops:
  7.2 0.7 all-gather.2.cloned.1.call-update
  8.1 21.2 %fusion = (f32[1024,1280]{0,1:T(8,128)}, f32[1024,1280]{0,1:T(8,128)}) fusion(f32[1280]{0:T(1024)S(1)} %fusion.19, f32[1024]{0:T(1024)S(1)} %convert_element_type.24, pred[1280]{0:T(1024)(128)(4,1)S(1)} %fusion.13), kind=kLoop, calls=%fused_computation.2 | loop fusion | flops 3932160 | bytes 10496256 | tf_op jit(solution)/shard_map/jit(_where)/select_n | solution.py:26
  29.2 11.9 %slice.17 = f32[1024,640]{0,1:T(8,128)} slice(f32[1024,1280]{0,1:T(8,128)} %get-tuple-element.12), slice={[0:1024:1], [0:1280:2]} | slice | bytes 5242880 | tf_op jit(solution)/shard_map/slice | solution.py:28
  41.2 4.9 copy.10
  46.1 7.5 %reshape.77 = f32[1024,640,2]{0,2,1:T(2,128)} reshape(f32[1024,1280]{0,1:T(8,128)} %copy.10) | data formatting | bytes 10485760 | tf_op jit(solution)/shard_map/reshape | solution.py:38
  53.7 11.9 %slice.15 = f32[1024,640]{0,1:T(8,128)} slice(f32[1024,1280]{0,1:T(8,128)} %get-tuple-element.11), slice={[0:1024:1], [0:1280:2]} | slice | bytes 5242880 | tf_op jit(solution)/shard_map/slice | solution.py:28
  65.6 10.9 %fusion.25 = (f32[1024,640,1]{0,2,1:T(1,128)}, f32[1024,640,1]{0,2,1:T(1,128)}) fusion(f32[1024,640,2]{0,2,1:T(2,128)} %reshape.77), kind=kLoop, calls=%fused_computation.49 | loop fusion | bytes 10485760 | tf_op jit(solution)/shard_map/slice | solution.py:39
  76.5 6.1 fusion.7
  82.6 0.2 pad_maximum_fusion
  82.9 4.2 copy.14
  87.1 5.3 convert_element_type.26
  92.3 110.9 %all-gather.2.cloned.1.call-done = bf16[8192,1280]{1,0:T(8,128)(2,1)} async-done(((bf16[2048,1280]{1,0:T(8,128)(2,1)}), bf16[8192,1280]{1,0:T(8,128)(2,1)}) %all-gather.2.cloned.1.call-update) | async-done | bytes 20971536 | tf_op jit(solution)/shard_map/all_gather | solution.py:56
  203.2 29.1 %fusion.26 = f32[1024,8192]{1,0:T(8,128)} fusion(bf16[1024,1280]{0,1:T(8,128)(2,1)} %convert_element_type.26, bf16[8192,1280]{1,0:T(8,128)(2,1)} %all-gather.2.cloned.1.call-done), kind=kOutput, calls=%fused_computation.50 | convolution fusion | flops 21474836480 | bytes 57147392 | tf_op jit(solution)/shard_map/dot_general | solution.py:54
  232.4 0.7 copy-done.2
  233.1 2.2 fusion.28
  235.3 0.7 fusion.27
  236.0 48.2 %all-reduce.6 = (bf16[1024,16]{0,1:T(8,128)(2,1)S(1)}, bf16[1024,16]{1,0:T(8,128)(2,1)S(1)}) all-reduce(f32[1024,16]{0,1:T(8,128)S(1)} %fusion.28, f32[1024,16]{1,0:T(8,128)S(1)} %fusion.27), channel_id=1, replica_groups=mesh['dp'=4,'tensor'=8] {'tensor'}, use_global_device_ids=true, to_apply=%region_1.2 | all-reduce | flops 32768 | bytes 196608 | tf_op jit(solution)/shard_map/psum | solution.py:48
  284.2 1.0 fusion.8
  285.2 3.2 convolution_multiply_fusion
  288.5 280.9 %reduce-scatter.2.cloned.1.call-done = f32[1024,1024]{1,0:T(8,128)} async-done(((f32[1024,8192]{1,0:T(8,128)}), f32[1024,1024]{1,0:T(8,128)}) %reduce-scatter.2.cloned.1.call-update) | async-done | bytes 4194320 | tf_op jit(solution)/shard_map/reduce_scatter | solution.py:59
  569.4 4.2 add_convert_fusion
  573.7 39.9 %all-reduce.5.cloned.1.call-done = (f32[1024,16]{0,1:T(8,128)}, f32[16,1280]{1,0:T(8,128)}) async-done(((f32[1024,16]{0,1:T(8,128)}, f32[16,1280]{1,0:T(8,128)}), (f32[1024,16]{0,1:T(8,128)}, f32[16,1280]{1,0:T(8,128)})) %all-reduce.5.cloned.1.call-update) | async-done | bytes 147472 | tf_op jit(solution)/shard_map/psum | solution.py:64
  613.6 1.5 copy.36
  615.0 1.5 copy.37
  (15 shorter events, 0.3 us)
Async XLA Ops:
  7.2 228.1 %copy-start = (bf16[1024,1024]{1,0:T(8,128)(2,1)S(1)}, bf16[1024,1024]{1,0:T(8,128)(2,1)}, u32[]{:S(2)}) copy-start(bf16[1024,1024]{1,0:T(8,128)(2,1)} %param.6) | copy-start | bytes 6291460
  7.2 0.8 copy-start.3
  7.2 196.0 %all-gather.2.cloned.1.call-start = ((), (), s32[]{:S(2)}) async-start(), calls=%async_computation.1 | async-start | bytes 26214400 | tf_op jit(solution)/shard_map/all_gather | solution.py:56
  7.9 561.5 %reduce-scatter.2.cloned.1.call-start = ((), (), s32[]{:S(2)}) async-start(), calls=%async_computation.2 | async-start | bytes 37748736 | tf_op jit(solution)/shard_map/reduce_scatter | solution.py:59
  232.3 0.8 copy-start.2
  232.3 2.9 copy-start.1
  232.4 381.2 %all-reduce.5.cloned.1.call-start = ((), (), s32[]{:S(2)}) async-start(), calls=%async_computation.3 | async-start | bytes 294912 | tf_op jit(solution)/shard_map/psum | solution.py:64
Sparse Core Ops, SparseCore 0:
  9.9 193.3 all-gather.1
  232.5 336.9 reduce-scatter.1
  573.0 40.5 all-reduce.4
where the time goes:
time: 627 us; the launch traced here: 623 us
  waiting for transfers between devices  432 us (69%)
  local copies, waits for them, and re-layouts  60.5 us (10%)
  blocking collectives  48.2 us (8%)
  matrix products  40.4 us (6%)
  other arithmetic  27.6 us (4%)
  between operations  13.8 us (2%)
    reduce_scatter x1, waiting for transfers between devices, on_device(): base = lax.psum_scatter(terms, 'tensor', scatter_dimension=1, tiled=True)  281 us
    all_gather x1, waiting for transfers between devices, on_device(): lax.all_gather(fixed_weight_matrix, 'dp', axis=0, tiled=True)  111 us
    psum x1, blocking collectives, on_device(): rank_input, rank_gradient = lax.psum((rank_input, rank_gradient), 'tensor')  48.2 us
    psum x1, waiting for transfers between devices, on_device(): grad_a, grad_b = lax.psum((part_a, part_b), 'dp')  39.9 us
    dot_general x1, matrix products, on_device(): jnp.dot(unrotated_gradient, lax.all_gather(fixed_weight_matrix, 'dp', axi...  29.1 us
    slice x2, local copies, waits for them, and re-layouts, rope_tables(): return (cosine[:, 0::2], sine[:, 0::2])  23.9 us
    select_n x1, other arithmetic, rope_tables(): cosine = jnp.where(rotate, jnp.cos(angle), jnp.float32(1.0))  21.2 us
  transfers between devices with their start and end apart: 3, of which 3 were waited for; matrix products, arithmetic and copies ran while one was open for 15% of the time, Pallas kernels for 0%

commit v1 on v0

v1 whole, which is shorter than its diff:
```python
import functools
import math

import jax
import jax.numpy as jnp
from jax import lax
from jax.experimental import pallas as pl
from jax.experimental.pallas import tpu as pltpu
from jax.sharding import PartitionSpec as P

MODEL_WIDTH = 8192
KV = 1024
HEAD = 128
MESH = pl.DeviceIdType.MESH


def rope_tables(positions, width, shards, shard):
    q_width = MODEL_WIDTH // shards
    k_width = KV // shards
    lane = jnp.arange(HEAD, dtype=jnp.int32)
    pair = (lane // 2).astype(jnp.float32)
    freq = jnp.float32(500000.0) ** (-2.0 * pair / HEAD)
    angle = positions.astype(jnp.float32)[:, None] * freq[None, :]
    cosine = jnp.cos(angle)
    sine = jnp.where(lane % 2 == 0, jnp.sin(angle), -jnp.sin(angle))
    return cosine, sine


def widen(table, width, shards, shard, fill):
    q_width = MODEL_WIDTH // shards
    k_width = KV // shards
    rows = table.shape[0]
    query = jnp.tile(table, (1, q_width // HEAD))
    if k_width % HEAD == 0:
        key = jnp.tile(table, (1, k_width // HEAD))
    else:
        key = lax.dynamic_slice_in_dim(
            jnp.tile(table, (1, 2 + k_width // HEAD)), (shard * k_width) % HEAD, k_width, 1
        )
    rest = jnp.full((rows, width - q_width - k_width), fill, jnp.float32)
    return jnp.concatenate([query, key, rest], axis=1)


def unrotate(gradient, positions, shards, shard):
    rows, width = gradient.shape
    cosine, sine = rope_tables(positions, width, shards, shard)
    cosine = widen(cosine, width, shards, shard, 1.0)
    sine = widen(sine, width, shards, shard, 0.0)
    grad = gradient.astype(jnp.float32)
    even = (jnp.arange(width, dtype=jnp.int32) % 2 == 0)[None, :]
    other = jnp.where(even, jnp.roll(grad, -1, axis=1), jnp.roll(grad, 1, axis=1))
    return (grad * cosine + other * sine).astype(jnp.bfloat16)


def base_kernel(
    sizes, gy, w, out, wbuf, prx, psend, zrx, pend,
    load_sem, wsend_sem, wrecv_sem, relay_sem, psend_sem, prx_sem, zsend_sem, zrx_sem,
):
    D, K, FB, TB, NT, RS, RP = sizes
    Z = D
    N = D * K * NT
    d = lax.axis_index("dp")
    t = lax.axis_index("tensor")
    z = t // 2
    core = t % 2
    partner = t + 1 - 2 * core
    relay = D == 4
    direct = (1, 2) if relay else tuple(range(1, D))

    def owner_at(r):
        if relay:
            x = (d % 2 + r % 2) % 2
            y = (d // 2 + r // 2) % 2
            return 2 * y + x
        return (d + r) % D

    def target_of(r):
        return owner_at(r) if relay else (d + D - r) % D

    def place(ci):
        if D < 4:
            return ci // K, ci % K
        mid = ci - K
        inter = jnp.logical_and(ci >= K, ci < 3 * K)
        r = jnp.where(inter, 1 + (mid + 2 * K) % 2, ci // K)
        k = jnp.where(inter, (mid + 2 * K) // 2 - K, ci % K)
        return r, k

    barrier = pltpu.get_barrier_semaphore()
    pl.semaphore_signal(barrier, inc=1, device_id={"tensor": partner}, device_id_type=MESH)
    for r in direct:
        pl.semaphore_signal(barrier, inc=1, device_id={"dp": target_of(r)}, device_id_type=MESH)

    @pl.when(z > 0)
    def _():
        pl.semaphore_signal(barrier, inc=1, device_id={"tensor": t - 2}, device_id_type=MESH)

    @pl.when(z < Z - 1)
    def _():
        pl.semaphore_signal(barrier, inc=1, device_id={"tensor": t + 2}, device_id_type=MESH)

    loads = pltpu.make_async_copy(w, wbuf.at[0], load_sem)
    loads.start()
    ends = jnp.where(z == 0, 1, 0) + jnp.where(z == Z - 1, 1, 0)
    pl.semaphore_wait(barrier, 3 + len(direct) - ends)
    loads.wait()

    def piece(r, k):
        return wbuf.at[r, :, pl.ds(k * FB, FB), :]

    def own_copy(r, k):
        return pltpu.make_async_remote_copy(
            src_ref=piece(0, k), dst_ref=piece(r, k),
            send_sem=wsend_sem.at[r, k], recv_sem=wrecv_sem.at[r, k],
            device_id={"dp": target_of(r)}, device_id_type=MESH,
        )

    def relay_copy(r, k):
        other = 3 - r
        return pltpu.make_async_remote_copy(
            src_ref=piece(r, k), dst_ref=piece(3, k),
            send_sem=relay_sem.at[k], recv_sem=wrecv_sem.at[3, k],
            device_id={"dp": target_of(other)}, device_id_type=MESH,
        )

    for k in range(K):
        for r in direct:
            own_copy(r, k).start()

    def partner_copy(it):
        return pltpu.make_async_remote_copy(
            src_ref=psend.at[it % RS], dst_ref=prx.at[it],
            send_sem=psend_sem.at[it % RS], recv_sem=prx_sem.at[it],
            device_id={"tensor": partner}, device_id_type=MESH,
        )

    def extra_slot(j):
        r, k = place(j // NT)
        return N + k * NT + j % NT

    def line_copy(j):
        r, k = place(j // NT)
        p = owner_at(r)
        slot = jnp.where(p == z - 1, extra_slot(j), j)
        return pltpu.make_async_remote_copy(
            src_ref=prx.at[j], dst_ref=zrx.at[slot],
            send_sem=zsend_sem.at[j], recv_sem=zrx_sem.at[slot],
            device_id={"tensor": t + jnp.where(p > z, 2, -2)}, device_id_type=MESH,
        )

    def arrived(slot):
        return pltpu.make_async_copy(zrx.at[slot], zrx.at[slot], zrx_sem.at[slot])

    def produce(it):
        ci = it // NT
        tb = it % NT
        r, k = place(ci)

        @pl.when(jnp.logical_and(tb == 0, r > 0))
        def _():
            pltpu.make_async_copy(piece(r, k), piece(r, k), wrecv_sem.at[r, k]).wait()
            if relay:
                first = jnp.logical_and(r == 2, k < K // 2)
                second = jnp.logical_and(r == 1, k >= K // 2)

                @pl.when(jnp.logical_or(first, second))
                def _():
                    relay_copy(r, k).start()

        @pl.when(it >= RS)
        def _():
            partner_copy(it - RS).wait_send()

        rows = gy[pl.ds(pl.multiple_of(tb * TB, TB), TB), :]

        def half(which):
            return lax.dot_general(
                rows, wbuf[r, which, pl.ds(pl.multiple_of(k * FB, FB), FB), :],
                (((1,), (1,)), ((), ())), preferred_element_type=jnp.float32,
            )

        psend[it % RS] = half(1 - core).astype(jnp.bfloat16)
        partner_copy(it).start()
        pend[it % RP] = half(core)

    def consume(j):
        r, k = place(j // NT)
        tb = j % NT
        p = owner_at(r)
        partner_copy(j).wait_recv()
        pend[j % RP] += prx[j].astype(jnp.float32)

        @pl.when(jnp.logical_and(z <= p, z > 0))
        def _():
            arrived(j).wait()
            pend[j % RP] += zrx[j].astype(jnp.float32)

        @pl.when(jnp.logical_and(z >= p, z < Z - 1))
        def _():
            slot = jnp.where(p == z, extra_slot(j), j)
            arrived(slot).wait()
            pend[j % RP] += zrx[slot].astype(jnp.float32)

        @pl.when(p == z)
        def _():
            out[k, pl.ds(pl.multiple_of(tb * TB, TB), TB), :] = pend[j % RP]

        @pl.when(p != z)
        def _():
            prx[j] = pend[j % RP].astype(jnp.bfloat16)
            line_copy(j).start()

    def upstream(j):
        p = owner_at(place(j // NT)[0])
        low, high = z, Z - 1 - z
        return jnp.where(z < p, low, jnp.where(z > p, high, jnp.maximum(low, high)))

    @pl.loop(0, N + Z)
    def _(it):
        @pl.when(it < N)
        def _():
            produce(it)

        @pl.loop(0, Z)
        def _(u):
            j = it - 1 - u
            inside = jnp.logical_and(j >= 0, j < N)
            safe = jnp.clip(j, 0, N - 1)

            @pl.when(jnp.logical_and(inside, upstream(safe) == u))
            def _():
                consume(safe)

    for k in range(K):
        for r in direct:
            own_copy(r, k).wait_send()
        if relay:
            relay_copy(2 if k < K // 2 else 1, k).wait_send()

    @pl.loop(N - RS, N)
    def _(it):
        partner_copy(it).wait_send()

    @pl.loop(0, N)
    def _(j):
        @pl.when(owner_at(place(j // NT)[0]) != z)
        def _():
            line_copy(j).wait_send()


def base_sum(gy, w, D):
    M, cols = gy.shape
    half = w.shape[0] // 2
    FB = min(256, half)
    TB = min(512, M)
    K, NT = half // FB, M // TB
    N = D * K * NT
    RS, RP = 4, D + 1
    dma = pltpu.SemaphoreType.DMA
    out = pl.pallas_call(
        functools.partial(base_kernel, (D, K, FB, TB, NT, RS, RP)),
        out_shape=jax.ShapeDtypeStruct((K, M, FB), jnp.float32),
        in_specs=[pl.BlockSpec(memory_space=pltpu.VMEM), pl.BlockSpec(memory_space=pl.ANY)],
        out_specs=pl.BlockSpec(memory_space=pltpu.VMEM),
        scratch_shapes=[
            pltpu.VMEM((D, 2, half, cols), jnp.bfloat16),
            pltpu.VMEM((N, TB, FB), jnp.bfloat16),
            pltpu.VMEM((RS, TB, FB), jnp.bfloat16),
            pltpu.VMEM((N + K * NT, TB, FB), jnp.bfloat16),
            pltpu.VMEM((RP, TB, FB), jnp.float32),
            dma,
            dma((D, K)),
            dma((D, K)),
            dma((K,)),
            dma((RS,)),
            dma((N,)),
            dma((N,)),
            dma((N + K * NT,)),
        ],
        compiler_params=pltpu.CompilerParams(
            collective_id=0, has_side_effects=True, vmem_limit_bytes=60 * 1024 * 1024
        ),
    )(gy, w.reshape(2, half, cols))
    return out.transpose(1, 0, 2).reshape(M, half)


def on_device(
    normed_input, positions, fixed_weight_matrix, adapter_down_map, adapter_up_map, output_gradient
):
    rows, width = output_gradient.shape
    shards = lax.axis_size("tensor")
    shard = lax.axis_index("tensor")
    D = lax.axis_size("dp")
    unrotated_gradient = unrotate(output_gradient, positions, shards, shard)
    rank_input = jnp.dot(normed_input, adapter_down_map, preferred_element_type=jnp.float32)
    rank_gradient = jnp.dot(
        unrotated_gradient, adapter_up_map.T, preferred_element_type=jnp.float32
    )
    if shards == 2 * D and D & (D - 1) == 0:
        base = base_sum(unrotated_gradient, fixed_weight_matrix, D)
    else:
        terms = jnp.dot(
            unrotated_gradient,
            lax.all_gather(fixed_weight_matrix, "dp", axis=0, tiled=True).T,
            preferred_element_type=jnp.float32,
        )
        base = lax.psum_scatter(terms, "tensor", scatter_dimension=1, tiled=True)
    rank_input, rank_gradient = lax.psum((rank_input, rank_gradient), "tensor")
    low_xb = rank_input.astype(jnp.bfloat16)
    rank_gradient_up = rank_gradient.astype(jnp.bfloat16)
    factor = 2.0 / math.sqrt(rows * D)
    part_a = factor * jnp.dot(normed_input.T, rank_gradient_up, preferred_element_type=jnp.float32)
    part_b = factor * jnp.dot(low_xb.T, unrotated_gradient, preferred_element_type=jnp.float32)
    adapter_branch = jnp.dot(
        rank_gradient_up, adapter_down_map.T, preferred_element_type=jnp.float32
    )
    grad_x = (base + 2.0 * adapter_branch).astype(jnp.bfloat16)
    grad_a, grad_b = lax.psum((part_a, part_b), "dp")
    return (grad_x, grad_a, grad_b)


def solution(mesh):
    placed = (
        P("dp", "tensor"),
        P("dp"),
        P("dp", "tensor"),
        P("tensor", None),
        P(None, "tensor"),
        P("dp", "tensor"),
    )
    return jax.shard_map(
        on_device,
        mesh=mesh,
        in_specs=placed,
        out_specs=(P("dp", "tensor"), P("tensor", None), P(None, "tensor")),
        check_vma=False,
    )
```

time: 627 us -> 333 us (0.53)
  waiting for transfers between devices: 432 us -> 0.02 us
  Pallas kernels: 0 us -> 236 us
  local copies, waits for them, and re-layouts: 60.5 us -> 29.5 us
  matrix products: 40.4 us -> 9.58 us
  other arithmetic: 27.6 us -> 7.41 us
  blocking collectives: 48.2 us -> 35.8 us
    reduce_scatter x1 -> x0, waiting for transfers between devices: 281 us -> none  [on_device(): base = lax.psum_scatter(terms, 'tensor', scatter_dimension=1, tiled=True)]
    pallas_call x0 -> x1, Pallas kernels: none -> 236 us  [base_sum(): pl.pallas_call(functools.partial(base_kernel, (D, K, FB, TB, NT, RS, RP))...]
    all_gather x1 -> x0, waiting for transfers between devices: 111 us -> none  [on_device(): lax.all_gather(fixed_weight_matrix, 'dp', axis=0, tiled=True)]
    psum x1, waiting for transfers between devices: 39.9 us -> 0.01 us  [on_device(): grad_a, grad_b = lax.psum((part_a, part_b), 'dp')]
    slice x3 -> x2, local copies, waits for them, and re-layouts: 34.8 us -> 4.13 us  [unrotate(): jnp.roll(grad, 1, axis=1)]
    dot_general x1 -> x0, matrix products: 29.1 us -> none  [on_device(): jnp.dot(unrotated_gradient, lax.all_gather(fixed_weight_matrix, 'dp', axi...]
    select_n x1, other arithmetic: 21.2 us -> 1.92 us  [rope_tables(): sine = jnp.where(lane % 2 == 0, jnp.sin(angle), -jnp.sin(angle))]
    psum x1, blocking collectives: 48.2 us -> 35.8 us  [on_device(): rank_input, rank_gradient = lax.psum((rank_input, rank_gradient), 'tensor')]
  transfers between devices with their start and end apart: 3 -> 1, of which waited for: 3 -> 0; matrix products, arithmetic and copies ran while one was open for 15% -> 5% of each run, Pallas kernels for 0% -> 71%
where the time goes in v1:
time: 333 us; the launch traced here: 332 us
  Pallas kernels  236 us (71%)
  blocking collectives  35.8 us (11%)
  local copies, waits for them, and re-layouts  29.5 us (9%)
  between operations  14.2 us (4%)
  matrix products  9.58 us (3%)
  other arithmetic  7.41 us (2%)
    pallas_call x1, Pallas kernels, base_sum(): pl.pallas_call(functools.partial(base_kernel, (D, K, FB, TB, NT, RS, RP))...  236 us
    psum x1, blocking collectives, on_device(): rank_input, rank_gradient = lax.psum((rank_input, rank_gradient), 'tensor')  35.8 us
    another operation x3, local copies, waits for them, and re-layouts, widen(): query = jnp.tile(table, (1, q_width // HEAD))  10 us
  transfers between devices with their start and end apart: 1, of which 0 were waited for; matrix products, arithmetic and copies ran while one was open for 5% of the time, Pallas kernels for 71%

profile of v1, /device:TPU:6, one launch (start us, length us, event | category | flops | bytes accessed | tf_op | source)
XLA Modules:
  0.0 332.5 jit_solution(1115718763761259015)
XLA Ops:
  7.2 0.0 copy-start
  7.2 0.0 all-reduce.5.cloned.1.call-start
  7.3 0.0 copy-start.1
  7.3 0.0 copy-start.5
  7.3 4.0 %fusion.16 = (f32[1024,1279]{1,0:T(8,128)S(1)}, f32[1024,1279]{1,0:T(8,128)S(1)}) fusion(bf16[1024,1280]{1,0:T(8,128)(2,1)} %param.11), kind=kLoop, calls=%fused_computation.33 | loop fusion | bytes 20955136 | tf_op jit(solution)/shard_map/jit(_roll_static)/slice | solution.py:51
  11.3 0.1 fusion.15
  11.5 1.9 negate_select_fusion
  13.4 0.3 tile.8
  13.7 2.2 tile.20
  15.9 7.6 %copy_bitcast_fusion = (f32[1024,1024]{1,0:T(8,128)}, f32[1024,1024]{1,0:T(8,128)}) fusion(f32[128,8,8,128]{3,2,1,0:T(8,128)} %bitcast.24, f32[128,8,8,128]{3,2,1,0:T(8,128)S(1)} %bitcast.23), kind=kLoop, calls=%fused_computation.5 | loop fusion | bytes 16777216 | tf_op jit(solution)/shard_map/tile | solution.py:33
  23.5 5.5 %fusion.1.gy = bf16[1024,1280]{1,0:T(8,128)(2,1)S(1)} fusion(f32[1024,128]{1,0:T(8,128)S(1)} %get-tuple-element.12, f32[1024,1024]{1,0:T(8,128)} %get-tuple-element.14, f32[1024,1]{1,0:T(8,128)S(1)} %get-tuple-element.8, f32[1024,1279]{1,0:T(8,128)S(1)} %get-tuple-element.10, f32[1024,1279]{1,0:T(8,128)S(1)} %get-tuple-element.9, ...), kind=kLoop, calls=%fused_computation.2 | loop fusion | flops 15728640 | bytes 25177344 | tf_op jit(solution)/shard_map/convert_element_type | solution.py:52
  29.0 1.5 copy-done.2
  30.5 0.8 fusion.17
  31.3 0.7 fusion.18
  32.0 35.8 %all-reduce.6 = (bf16[1024,16]{0,1:T(8,128)(2,1)S(1)}, bf16[1024,16]{1,0:T(8,128)(2,1)S(1)}) all-reduce(f32[1024,16]{0,1:T(8,128)S(1)} %fusion.17, f32[1024,16]{1,0:T(8,128)S(1)} %fusion.18), channel_id=1, replica_groups=mesh['dp'=4,'tensor'=8] {'tensor'}, use_global_device_ids=true, to_apply=%region_0.1 | all-reduce | flops 32768 | bytes 196608 | tf_op jit(solution)/shard_map/psum | solution.py:308
  67.8 2.9 convolution_multiply_fusion
  70.6 1.0 fusion.3
  71.7 0.0 all-reduce.5.cloned.1.call-update
  71.7 236.0 %shard_map.85 = f32[4,1024,256]{2,1,0:T(8,128)} custom-call(bf16[1024,1280]{1,0:T(8,128)(2,1)} %copy-done.2, bf16[2,1024,1280]{2,1,0:T(8,128)(2,1)} %bitcast.25), custom_call_target="tpu_custom_call" | custom-call | tf_op jit(solution)/shard_map/pallas_call | solution.py:260
  307.6 5.4 %copy.9 = f32[1024,4,256]{0,2,1:T(8,128)} copy(f32[1024,4,256]{2,0,1:T(8,128)} %bitcast.21) | data formatting | bytes 8388608 | tf_op jit(solution)/shard_map/transpose | solution.py:284
  313.0 5.4 %copy.10 = f32[1024,1024]{1,0:T(8,128)} copy(f32[1024,1024]{0,1:T(8,128)} %bitcast.22) | data formatting | bytes 8388608 | tf_op jit(solution)/shard_map/reshape | solution.py:284
  318.4 4.2 %add_convert_fusion = bf16[1024,1024]{1,0:T(8,128)(2,1)} fusion(f32[1024,1024]{1,0:T(8,128)} %copy.10, bf16[1024,16]{0,1:T(8,128)(2,1)S(1)} %copy-done.3, bf16[1024,16]{0,1:T(8,128)(2,1)S(1)} %get-tuple-element.3), kind=kOutput, calls=%fused_computation.7 | convolution fusion | flops 36700160 | bytes 6356992 | tf_op jit(solution)/shard_map/dot_general | solution.py:314
  322.6 1.5 copy.21
  324.1 1.5 copy.22
  (17 shorter events, 0.1 us)
Async XLA Ops:
  7.2 24.1 %copy-start = (bf16[1024,1024]{1,0:T(8,128)(2,1)S(1)}, bf16[1024,1024]{1,0:T(8,128)(2,1)}, u32[]{:S(2)}) copy-start(bf16[1024,1024]{1,0:T(8,128)(2,1)} %param.6) | copy-start | bytes 6291460
  7.2 315.5 %all-reduce.5.cloned.1.call-start = ((), (), s32[]{:S(2)}) async-start(), calls=%async_computation | async-start | bytes 294912 | tf_op jit(solution)/shard_map/psum | solution.py:318
  7.3 4.0 %copy-start.1 = (bf16[1024,1280]{1,0:T(8,128)(2,1)S(1)}, bf16[1024,1280]{1,0:T(8,128)(2,1)}, u32[]{:S(2)}) copy-start(bf16[1024,1280]{1,0:T(8,128)(2,1)} %param.11) | copy-start | bytes 7864324
  7.3 4.2 %copy-start.5 = (s32[1024]{0:T(1024)S(1)}, s32[1024]{0:T(1024)}, u32[]{:S(2)}) copy-start(s32[1024]{0:T(1024)} %param.7) | copy-start | bytes 12292
  23.5 7.0 %copy-start.4 = (bf16[16,1280]{1,0:T(8,128)(2,1)S(1)}, bf16[16,1280]{1,0:T(8,128)(2,1)}, u32[]{:S(2)}) copy-start(bf16[16,1280]{1,0:T(8,128)(2,1)} %param.10) | copy-start | bytes 122884
  23.5 7.8 %copy-start.3 = (bf16[1024,16]{0,1:T(8,128)(2,1)S(1)}, bf16[1024,16]{0,1:T(8,128)(2,1)}, u32[]{:S(2)}) copy-start(bf16[1024,16]{0,1:T(8,128)(2,1)} %param.9) | copy-start | bytes 98308
  29.0 1.5 copy-start.2
Sparse Core Ops, SparseCore 0:
  71.8 40.7 all-reduce.4

commit v2 on v1

v2 whole, which is shorter than its diff:
```python
import functools
import math

import jax
import jax.numpy as jnp
from jax import lax
from jax.experimental import pallas as pl
from jax.experimental.pallas import tpu as pltpu
from jax.sharding import PartitionSpec as P

MODEL_WIDTH = 8192
KV = 1024
HEAD = 128
MESH = pl.DeviceIdType.MESH


def rope_tables(positions, width, shards, shard):
    q_width = MODEL_WIDTH // shards
    k_width = KV // shards
    lane = jnp.arange(HEAD + width - q_width, dtype=jnp.int32)
    after = lane - HEAD
    rotate = after < k_width
    dimension = jnp.where(lane < HEAD, lane, (shard * k_width + after) % HEAD)
    pair = (dimension // 2).astype(jnp.float32)
    freq = jnp.float32(500000.0) ** (-2.0 * pair / HEAD)
    angle = positions.astype(jnp.float32)[:, None] * freq[None, :]
    cosine = jnp.where(rotate, jnp.cos(angle), jnp.float32(1.0))
    sine = jnp.where(lane % 2 == 0, jnp.sin(angle), -jnp.sin(angle))
    return cosine, jnp.where(rotate, sine, jnp.float32(0.0))


def fused_kernel(
    sizes, g, cosine, sine, x, down, down_wide, up, w,
    out, out_a, out_b,
    gy, wbuf, prx, psend, zrx, pend, low_part, low_rx, low_all, low_tall, ab_own, ab_send, ab_rx,
    load_sem, wsend_sem, wrecv_sem, relay_sem, psend_sem, prx_sem, zsend_sem, zrx_sem,
    low_s1, low_r1, low_s2, low_r2, ab_s, ab_r,
):
    D, K, FB, TB, RS, RP, factor = sizes
    Z = D
    T = 2 * D
    N = D * K
    M, cols = g.shape
    F = x.shape[1]
    L = M // T
    rank = up.shape[0]
    d = lax.axis_index("dp")
    t = lax.axis_index("tensor")
    z = t // 2
    core = t % 2
    partner = t + 1 - 2 * core
    relay = D == 4
    direct = (1, 2) if relay else tuple(range(1, D))

    def owner_at(r):
        if relay:
            xx = (d % 2 + r % 2) % 2
            yy = (d // 2 + r // 2) % 2
            return 2 * yy + xx
        return (d + r) % D

    def target_of(r):
        return owner_at(r) if relay else (d + D - r) % D

    def place(ci):
        if D < 4:
            return ci // K, ci % K
        mid = ci + K
        inter = jnp.logical_and(ci >= K, ci < 3 * K)
        r = jnp.where(inter, 1 + mid % 2, ci // K)
        k = jnp.where(inter, mid // 2 - K, ci % K)
        if relay:
            last = ci % K
            k = jnp.where(ci >= 3 * K, (last % 2) * (K // 2) + last // 2, k)
        return r, k

    barrier = pltpu.get_barrier_semaphore()
    for o in range(1, T):
        pl.semaphore_signal(
            barrier, inc=1, device_id={"tensor": (t + o) % T}, device_id_type=MESH
        )
    for o in range(1, D):
        pl.semaphore_signal(barrier, inc=1, device_id={"dp": (d + o) % D}, device_id_type=MESH)
    loads = pltpu.make_async_copy(w, wbuf.at[0], load_sem)
    loads.start()
    pl.semaphore_wait(barrier, T + D - 2)
    loads.wait()

    def piece(r, k):
        return wbuf.at[r, :, pl.ds(k * FB, FB), :]

    def own_copy(r, k):
        return pltpu.make_async_remote_copy(
            src_ref=piece(0, k), dst_ref=piece(r, k),
            send_sem=wsend_sem.at[r, k], recv_sem=wrecv_sem.at[r, k],
            device_id={"dp": target_of(r)}, device_id_type=MESH,
        )

    def relay_copy(r, k):
        return pltpu.make_async_remote_copy(
            src_ref=piece(r, k), dst_ref=piece(3, k),
            send_sem=relay_sem.at[k], recv_sem=wrecv_sem.at[3, k],
            device_id={"dp": target_of(3 - r)}, device_id_type=MESH,
        )

    for k in range(K):
        for r in direct:
            own_copy(r, k).start()

    step = 128

    @pl.loop(0, M // step)
    def _(i):
        rows = pl.ds(pl.multiple_of(i * step, step), step)
        even = lax.broadcasted_iota(jnp.int32, (step, HEAD), 1) % 2 == 0
        for c in range(cols // HEAD):
            at = pl.ds(c * HEAD, HEAD)
            tab = max(0, c * HEAD - MODEL_WIDTH // T + HEAD)
            tat = pl.ds(tab, HEAD)
            val = g[rows, at].astype(jnp.float32)
            other = jnp.where(even, pltpu.roll(val, HEAD - 1, 1), pltpu.roll(val, 1, 1))
            gy[rows, at] = (val * cosine[rows, tat] + other * sine[rows, tat]).astype(jnp.bfloat16)

    nt = (((1,), (1,)), ((), ()))
    for s in range(T):
        rows = pl.ds(s * L, L)
        low_part[s, :rank] = lax.dot_general(
            down[...], x[rows, :], nt, preferred_element_type=jnp.float32
        )
        low_part[s, rank:] = lax.dot_general(
            up[...], gy[rows, :], nt, preferred_element_type=jnp.float32
        )

    def low_scatter(o):
        to = (t + o) % T
        return pltpu.make_async_remote_copy(
            src_ref=low_part.at[to], dst_ref=low_rx.at[o],
            send_sem=low_s1.at[o], recv_sem=low_r1.at[o],
            device_id={"tensor": to}, device_id_type=MESH,
        )

    def low_gather(o):
        return pltpu.make_async_remote_copy(
            src_ref=low_all.at[t], dst_ref=low_all.at[t],
            send_sem=low_s2.at[o], recv_sem=low_r2.at[o],
            device_id={"tensor": (t + o) % T}, device_id_type=MESH,
        )

    def ab_copy(o):
        return pltpu.make_async_remote_copy(
            src_ref=ab_send, dst_ref=ab_rx.at[o],
            send_sem=ab_s.at[o], recv_sem=ab_r.at[o],
            device_id={"dp": (d + o) % D}, device_id_type=MESH,
        )

    for o in range(1, T):
        low_scatter(o).start()

    def low_reduce():
        total = low_part[t]
        for o in range(1, T):
            low_scatter(o).wait_recv()
            total += low_rx[o]
        low_all[t] = total.astype(jnp.bfloat16)
        for o in range(1, T):
            low_gather(o).start()

    def low_finish():
        for o in range(1, T):
            src = (t + T - o) % T
            pltpu.make_async_copy(low_all.at[src], low_all.at[src], low_r2.at[o]).wait()
        low = jnp.concatenate([low_all[s].astype(jnp.float32) for s in range(T)], axis=1)
        low_tall[...] = low.T.astype(jnp.bfloat16)
        low = low.astype(jnp.bfloat16)
        ab_own[:, :F] = jnp.dot(low[rank:], x[...], preferred_element_type=jnp.float32)
        ab_own[:, F:] = jnp.dot(low[:rank], gy[...], preferred_element_type=jnp.float32)
        ab_send[...] = ab_own[...].astype(jnp.bfloat16)
        for o in range(1, D):
            ab_copy(o).start()

    def partner_copy(it):
        return pltpu.make_async_remote_copy(
            src_ref=psend.at[it % RS], dst_ref=prx.at[it],
            send_sem=psend_sem.at[it % RS], recv_sem=prx_sem.at[it],
            device_id={"tensor": partner}, device_id_type=MESH,
        )

    def extra_slot(j):
        return N + place(j)[1]

    def line_copy(j):
        p = owner_at(place(j)[0])
        slot = jnp.where(p == z - 1, extra_slot(j), j)
        return pltpu.make_async_remote_copy(
            src_ref=prx.at[j], dst_ref=zrx.at[slot],
            send_sem=zsend_sem.at[j], recv_sem=zrx_sem.at[slot],
            device_id={"tensor": t + jnp.where(p > z, 2, -2)}, device_id_type=MESH,
        )

    def arrived(slot):
        return pltpu.make_async_copy(zrx.at[slot], zrx.at[slot], zrx_sem.at[slot])

    def produce(it):
        r, k = place(it)

        @pl.when(r > 0)
        def _():
            pltpu.make_async_copy(piece(r, k), piece(r, k), wrecv_sem.at[r, k]).wait()
            if relay:
                first = jnp.logical_and(r == 2, k < K // 2)
                second = jnp.logical_and(r == 1, k >= K // 2)

                @pl.when(jnp.logical_or(first, second))
                def _():
                    relay_copy(r, k).start()

        @pl.when(it >= RS)
        def _():
            partner_copy(it - RS).wait_send()

        @pl.loop(0, M // TB)
        def _(tb):
            rows = pl.ds(pl.multiple_of(tb * TB, TB), TB)
            rhs = wbuf[r, :, pl.ds(pl.multiple_of(k * FB, FB), FB), :].reshape(2 * FB, cols)
            both = lax.dot_general(gy[rows, :], rhs, nt, preferred_element_type=jnp.float32)
            zero, one = both[:, :FB], both[:, FB:]
            psend[it % RS, rows, :] = jnp.where(core == 0, one, zero).astype(jnp.bfloat16)
            pend[it % RP, rows, :] = jnp.where(core == 0, zero, one)

        partner_copy(it).start()

    def consume(j):
        r, k = place(j)
        p = owner_at(r)
        partner_copy(j).wait_recv()
        pend[j % RP] += prx[j].astype(jnp.float32)

        @pl.when(jnp.logical_and(z <= p, z > 0))
        def _():
            arrived(j).wait()
            pend[j % RP] += zrx[j].astype(jnp.float32)

        @pl.when(jnp.logical_and(z >= p, z < Z - 1))
        def _():
            slot = jnp.where(p == z, extra_slot(j), j)
            arrived(slot).wait()
            pend[j % RP] += zrx[slot].astype(jnp.float32)

        @pl.when(p == z)
        def _():
            at = pl.ds(pl.multiple_of(k * FB, FB), FB)
            extra = jnp.dot(low_tall[...], down_wide[:, at], preferred_element_type=jnp.float32)
            out[:, at] = (pend[j % RP] + 2.0 * extra).astype(jnp.bfloat16)

        @pl.when(p != z)
        def _():
            prx[j] = pend[j % RP].astype(jnp.bfloat16)
            line_copy(j).start()

    def upstream(j):
        p = owner_at(place(j)[0])
        low, high = z, Z - 1 - z
        return jnp.where(z < p, low, jnp.where(z > p, high, jnp.maximum(low, high)))

    @pl.loop(0, N + Z)
    def _(it):
        @pl.when(it < N)
        def _():
            produce(it)

        @pl.when(it == 1)
        def _():
            low_reduce()

        @pl.when(it == 2)
        def _():
            low_finish()

        @pl.loop(0, Z)
        def _(u):
            j = it - 1 - u
            inside = jnp.logical_and(j >= 0, j < N)
            safe = jnp.clip(j, 0, N - 1)

            @pl.when(jnp.logical_and(inside, upstream(safe) == u))
            def _():
                consume(safe)

    for o in range(1, D):
        ab_copy(o).wait_recv()
    total = ab_own[...]
    for o in range(1, D):
        total += ab_rx[o].astype(jnp.float32)
    total = factor * total
    out_a[...] = total[:, :F]
    out_b[...] = total[:, F:]

    for o in range(1, D):
        ab_copy(o).wait_send()
    for o in range(1, T):
        low_scatter(o).wait_send()
        low_gather(o).wait_send()
    for k in range(K):
        for r in direct:
            own_copy(r, k).wait_send()
        if relay:
            relay_copy(2 if k < K // 2 else 1, k).wait_send()

    @pl.loop(N - RS, N)
    def _(it):
        partner_copy(it).wait_send()

    @pl.loop(0, N)
    def _(j):
        @pl.when(owner_at(place(j)[0]) != z)
        def _():
            line_copy(j).wait_send()


def fused(x, positions, w, down_map, up, g, D):
    M, cols = g.shape
    T = 2 * D
    half = w.shape[0] // 2
    F = x.shape[1]
    rank = up.shape[0]
    FB = 128
    TB = min(512, M)
    K = half // FB
    N = D * K
    RS, RP = 4, D + 1
    factor = 2.0 / math.sqrt(M * D)
    cosine, sine = rope_tables(positions, cols, T, lax.axis_index("tensor"))
    down = down_map.T
    down_wide = jnp.concatenate([jnp.zeros_like(down), down], axis=0)
    dma = pltpu.SemaphoreType.DMA
    vmem = pl.BlockSpec(memory_space=pltpu.VMEM)
    f32, bf16 = jnp.float32, jnp.bfloat16
    out, out_a, out_b = pl.pallas_call(
        functools.partial(fused_kernel, (D, K, FB, TB, RS, RP, factor)),
        out_shape=(
            jax.ShapeDtypeStruct((M, half), bf16),
            jax.ShapeDtypeStruct((rank, F), f32),
            jax.ShapeDtypeStruct((rank, cols), f32),
        ),
        in_specs=[vmem] * 7 + [pl.BlockSpec(memory_space=pl.ANY)],
        out_specs=(vmem, vmem, vmem),
        scratch_shapes=[
            pltpu.VMEM((M, cols), bf16),
            pltpu.VMEM((D, 2, half, cols), bf16),
            pltpu.VMEM((N, M, FB), bf16),
            pltpu.VMEM((RS, M, FB), bf16),
            pltpu.VMEM((N + K, M, FB), bf16),
            pltpu.VMEM((RP, M, FB), f32),
            pltpu.VMEM((T, 2 * rank, M // T), f32),
            pltpu.VMEM((T, 2 * rank, M // T), f32),
            pltpu.VMEM((T, 2 * rank, M // T), bf16),
            pltpu.VMEM((M, 2 * rank), bf16),
            pltpu.VMEM((rank, F + cols), f32),
            pltpu.VMEM((rank, F + cols), bf16),
            pltpu.VMEM((D, rank, F + cols), bf16),
            dma,
            dma((D, K)),
            dma((D, K)),
            dma((K,)),
            dma((RS,)),
            dma((N,)),
            dma((N,)),
            dma((N + K,)),
            dma((T,)),
            dma((T,)),
            dma((T,)),
            dma((T,)),
            dma((D,)),
            dma((D,)),
        ],
        compiler_params=pltpu.CompilerParams(
            collective_id=0, has_side_effects=True, vmem_limit_bytes=63 * 1024 * 1024
        ),
    )(g, cosine, sine, x, down, down_wide, up, w.reshape(2, half, cols))
    return out, out_a.T, out_b


def on_device(x, positions, w, down_map, up, g):
    D = lax.axis_size("dp")
    return fused(x, positions, w, down_map, up, g, D)


def solution(mesh):
    placed = (
        P("dp", "tensor"),
        P("dp"),
        P("dp", "tensor"),
        P("tensor", None),
        P(None, "tensor"),
        P("dp", "tensor"),
    )
    return jax.shard_map(
        on_device,
        mesh=mesh,
        in_specs=placed,
        out_specs=(P("dp", "tensor"), P("tensor", None), P(None, "tensor")),
        check_vma=False,
    )
```

time: 333 us -> 232 us (0.70)
  blocking collectives: 35.8 us -> 0 us
  local copies, waits for them, and re-layouts: 29.5 us -> 5.78 us
  Pallas kernels: 236 us -> 217 us
  between operations: 14.2 us -> 0.67 us
  matrix products: 9.58 us -> 0 us
    psum x1 -> x0, blocking collectives: 35.8 us -> none  [on_device(): rank_input, rank_gradient = lax.psum((rank_input, rank_gradient), 'tensor')]
    pallas_call x1, Pallas kernels: 236 us -> 217 us  [fused(): pl.pallas_call(functools.partial(fused_kernel, (D, K, FB, TB, RS, RP, fac...]
    another operation x3 -> x0, local copies, waits for them, and re-layouts: 10 us -> none  [widen(): query = jnp.tile(table, (1, q_width // HEAD))]
    dot_general x5 -> x0, matrix products: 9.58 us -> none  [the longest x1 4.24 us: on_device(): jnp.dot(rank_gradient_up, adapter_down_map.T, preferred_element_type=jnp....]
    convert_element_type x1 -> x0, other arithmetic: 5.47 us -> none  [unrotate(): return (grad * cosine + other * sine).astype(jnp.bfloat16)]
    transpose x1 -> x0, local copies, waits for them, and re-layouts: 5.4 us -> none  [base_sum(): return out.transpose(1, 0, 2).reshape(M, half)]
    reshape x1 -> x0, local copies, waits for them, and re-layouts: 5.36 us -> none  [base_sum(): return out.transpose(1, 0, 2).reshape(M, half)]
    select_n x1, other arithmetic: 1.92 us -> 7.16 us  [rope_tables(): return (cosine, jnp.where(rotate, sine, jnp.float32(0.0)))]
  transfers between devices with their start and end apart: 1 -> 0, of which waited for: 0 -> 0; matrix products, arithmetic and copies ran while one was open for 5% -> 0% of each run, Pallas kernels for 71% -> 0%
where the time goes in v2:
time: 232 us
  Pallas kernels  217 us (94%)
  other arithmetic  7.89 us (3%)
  local copies, waits for them, and re-layouts  5.78 us (2%)
    pallas_call x1, Pallas kernels, fused(): pl.pallas_call(functools.partial(fused_kernel, (D, K, FB, TB, RS, RP, fac...  217 us
    select_n x1, other arithmetic, rope_tables(): return (cosine, jnp.where(rotate, sine, jnp.float32(0.0)))  7.16 us

profile of v2, /device:TPU:6, one launch (start us, length us, event | category | flops | bytes accessed | tf_op | source)
XLA Modules:
  0.0 231.7 jit_solution(12150257393916465919)
XLA Ops:
  0.7 0.7 convert_element_type.10
  1.4 1.4 concatenate.3.down_wide
  2.8 7.2 %fusion.1 = (f32[1024,384]{1,0:T(8,128)}, f32[1024,384]{1,0:T(8,128)}) fusion(f32[384]{0:T(512)S(1)} %fusion.7, f32[1024]{0:T(1024)S(1)} %convert_element_type.10, pred[384]{0:T(512)(128)(4,1)S(1)} %get-tuple-element.11, pred[384]{0:T(512)(128)(4,1)S(1)} %get-tuple-element.12), kind=kLoop, calls=%fused_computation.4 | loop fusion | flops 1966080 | bytes 3152128 | tf_op jit(solution)/shard_map/jit(_where)/select_n | solution.py:29
  9.9 217.4 %shard_map.85 = (bf16[1024,1024]{1,0:T(8,128)(2,1)}, f32[16,1024]{1,0:T(8,128)}, f32[16,1280]{1,0:T(8,128)}) custom-call(bf16[1024,1280]{1,0:T(8,128)(2,1)} %g.1, f32[1024,384]{1,0:T(8,128)} %get-tuple-element.10.cosine, f32[1024,384]{1,0:T(8,128)} %get-tuple-element.9.sine, bf16[1024,1024]{1,0:T(8,128)(2,1)} %x.3, bf16[16,1024]{1,0:T(8,128)(2,1)} %bitcast.5, ...), custom_call_target="tpu_custom_call" | custom-call | tf_op jit(solution)/shard_map/pallas_call | solution.py:338
  227.3 0.0 copy-start.1
  227.3 0.0 copy-start
  227.3 3.1 %copy.12 = bf16[1024,1024]{1,0:T(8,128)(2,1)} copy(bf16[1024,1024]{1,0:T(8,128)(2,1)} %get-tuple-element.16) | data formatting | bytes 4194304
  230.5 0.0 copy-done.1
  230.5 0.6 copy.13
  231.1 0.0 copy-done
  231.1 0.6 copy.14
  (2 shorter events, 0.0 us)
Async XLA Ops:
  227.3 3.1 %copy-start.1 = (f32[16,1024]{1,0:T(8,128)S(1)}, f32[16,1024]{1,0:T(8,128)}, u32[]{:S(2)}) copy-start(f32[16,1024]{1,0:T(8,128)} %get-tuple-element.7) | copy-start | bytes 196612
  227.3 3.8 %copy-start = (f32[16,1280]{1,0:T(8,128)S(1)}, f32[16,1280]{1,0:T(8,128)}, u32[]{:S(2)}) copy-start(f32[16,1280]{1,0:T(8,128)} %get-tuple-element.18) | copy-start | bytes 245764

commit v3 on v2

--- a/solution.py
+++ b/solution.py
@@ -14,25 +14,21 @@
 MESH = pl.DeviceIdType.MESH
 
 
-def rope_tables(positions, width, shards, shard):
+def rope_lanes(width, shards, shard):
     q_width = MODEL_WIDTH // shards
     k_width = KV // shards
     lane = jnp.arange(HEAD + width - q_width, dtype=jnp.int32)
     after = lane - HEAD
-    rotate = after < k_width
     dimension = jnp.where(lane < HEAD, lane, (shard * k_width + after) % HEAD)
     pair = (dimension // 2).astype(jnp.float32)
     freq = jnp.float32(500000.0) ** (-2.0 * pair / HEAD)
-    angle = positions.astype(jnp.float32)[:, None] * freq[None, :]
-    cosine = jnp.where(rotate, jnp.cos(angle), jnp.float32(1.0))
-    sine = jnp.where(lane % 2 == 0, jnp.sin(angle), -jnp.sin(angle))
-    return cosine, jnp.where(rotate, sine, jnp.float32(0.0))
+    return freq[None, :], (after < k_width).astype(jnp.float32)[None, :]
 
 
 def fused_kernel(
-    sizes, g, cosine, sine, x, down, down_wide, up, w,
+    sizes, g, positions, freq, rotates, x, down, down_wide, up, w,
     out, out_a, out_b,
-    gy, wbuf, prx, psend, zrx, pend, low_part, low_rx, low_all, low_tall, ab_own, ab_send, ab_rx,
+    gy, wbuf, prx, psend, zrx, pend, fin, low_part, low_rx, low_all, low_tall, ab_own, ab_send, ab_rx,
     load_sem, wsend_sem, wrecv_sem, relay_sem, psend_sem, prx_sem, zsend_sem, zrx_sem,
     low_s1, low_r1, low_s2, low_r2, ab_s, ab_r,
 ):
@@ -84,14 +80,13 @@
     loads = pltpu.make_async_copy(w, wbuf.at[0], load_sem)
     loads.start()
     pl.semaphore_wait(barrier, T + D - 2)
-    loads.wait()
 
     def piece(r, k):
         return wbuf.at[r, :, pl.ds(k * FB, FB), :]
 
     def own_copy(r, k):
         return pltpu.make_async_remote_copy(
-            src_ref=piece(0, k), dst_ref=piece(r, k),
+            src_ref=w.at[:, pl.ds(k * FB, FB), :], dst_ref=piece(r, k),
             send_sem=wsend_sem.at[r, k], recv_sem=wrecv_sem.at[r, k],
             device_id={"dp": target_of(r)}, device_id_type=MESH,
         )
@@ -108,18 +103,39 @@
             own_copy(r, k).start()
 
     step = 128
+    q_width, k_width = MODEL_WIDTH // T, KV // T
 
     @pl.loop(0, M // step)
     def _(i):
         rows = pl.ds(pl.multiple_of(i * step, step), step)
         even = lax.broadcasted_iota(jnp.int32, (step, HEAD), 1) % 2 == 0
-        for c in range(cols // HEAD):
-            at = pl.ds(c * HEAD, HEAD)
-            tab = max(0, c * HEAD - MODEL_WIDTH // T + HEAD)
-            tat = pl.ds(tab, HEAD)
+        place_of = jnp.broadcast_to(positions[rows, :].astype(jnp.float32), (step, HEAD))
+
+        def table(lanes):
+            angle = place_of * freq[:, lanes]
+            sine = jnp.sin(angle)
+            return jnp.cos(angle), jnp.where(even, sine, -sine)
+
+        head = table(pl.ds(0, HEAD))
+        for off in range(0, cols, HEAD):
+            at = pl.ds(off, HEAD)
+            cosine, sine = head
+            if off >= q_width:
+                if k_width % HEAD == 0:
+                    if off >= q_width + k_width:
+                        gy[rows, at] = g[rows, at]
+                        continue
+                else:
+                    tail = pl.ds(HEAD + off - q_width, HEAD)
+                    cosine, sine = table(tail)
+                    turn = jnp.broadcast_to(rotates[:, tail], (step, HEAD)) > 0.5
+                    cosine = jnp.where(turn, cosine, 1.0)
+                    sine = jnp.where(turn, sine, 0.0)
             val = g[rows, at].astype(jnp.float32)
             other = jnp.where(even, pltpu.roll(val, HEAD - 1, 1), pltpu.roll(val, 1, 1))
-            gy[rows, at] = (val * cosine[rows, tat] + other * sine[rows, tat]).astype(jnp.bfloat16)
+            gy[rows, at] = (val * cosine + other * sine).astype(jnp.bfloat16)
+
+    loads.wait()
 
     nt = (((1,), (1,)), ((), ()))
     for s in range(T):
@@ -229,53 +245,54 @@
 
         partner_copy(it).start()
 
-    def consume(j):
+    def forward(j):
         r, k = place(j)
         p = owner_at(r)
         partner_copy(j).wait_recv()
         pend[j % RP] += prx[j].astype(jnp.float32)
 
-        @pl.when(jnp.logical_and(z <= p, z > 0))
+        @pl.when(jnp.logical_and(z < p, z > 0))
         def _():
             arrived(j).wait()
             pend[j % RP] += zrx[j].astype(jnp.float32)
 
-        @pl.when(jnp.logical_and(z >= p, z < Z - 1))
-        def _():
-            slot = jnp.where(p == z, extra_slot(j), j)
-            arrived(slot).wait()
-            pend[j % RP] += zrx[slot].astype(jnp.float32)
+        @pl.when(jnp.logical_and(z > p, z < Z - 1))
+        def _():
+            arrived(j).wait()
+            pend[j % RP] += zrx[j].astype(jnp.float32)
 
         @pl.when(p == z)
         def _():
-            at = pl.ds(pl.multiple_of(k * FB, FB), FB)
-            extra = jnp.dot(low_tall[...], down_wide[:, at], preferred_element_type=jnp.float32)
-            out[:, at] = (pend[j % RP] + 2.0 * extra).astype(jnp.bfloat16)
+            fin[k] = pend[j % RP]
 
         @pl.when(p != z)
         def _():
             prx[j] = pend[j % RP].astype(jnp.bfloat16)
             line_copy(j).start()
 
+    def finish(j):
+        k = place(j)[1]
+        at = pl.ds(pl.multiple_of(k * FB, FB), FB)
+
+        @pl.when(z > 0)
+        def _():
+            arrived(j).wait()
+            fin[k] += zrx[j].astype(jnp.float32)
+
+        @pl.when(z < Z - 1)
+        def _():
+            arrived(N + k).wait()
+            fin[k] += zrx[N + k].astype(jnp.float32)
+
+        extra = jnp.dot(low_tall[...], down_wide[:, at], preferred_element_type=jnp.float32)
+        out[:, at] = (fin[k] + 2.0 * extra).astype(jnp.bfloat16)
+
     def upstream(j):
         p = owner_at(place(j)[0])
-        low, high = z, Z - 1 - z
-        return jnp.where(z < p, low, jnp.where(z > p, high, jnp.maximum(low, high)))
+        return jnp.where(z < p, z, jnp.where(z > p, Z - 1 - z, 0))
 
     @pl.loop(0, N + Z)
     def _(it):
-        @pl.when(it < N)
-        def _():
-            produce(it)
-
-        @pl.when(it == 1)
-        def _():
-            low_reduce()
-
-        @pl.when(it == 2)
-        def _():
-            low_finish()
-
         @pl.loop(0, Z)
         def _(u):
             j = it - 1 - u
@@ -284,7 +301,31 @@
 
             @pl.when(jnp.logical_and(inside, upstream(safe) == u))
             def _():
-                consume(safe)
+                forward(safe)
+
+        @pl.when(it < N)
+        def _():
+            produce(it)
+
+        @pl.when(it == 1)
+        def _():
+            low_reduce()
+
+        @pl.when(it == 2)
+        def _():
+            low_finish()
+
+        @pl.loop(0, 2)
+        def _(end):
+            j = it - jnp.where(end == 1, Z, Z + K)
+            inside = jnp.logical_and(
+                jnp.logical_and(j >= 0, j < N), (j >= N - K) == (end == 1)
+            )
+            safe = jnp.clip(j, 0, N - 1)
+
+            @pl.when(jnp.logical_and(inside, owner_at(place(safe)[0]) == z))
+            def _():
+                finish(safe)
 
     for o in range(1, D):
         ab_copy(o).wait_recv()
@@ -327,9 +368,9 @@
     TB = min(512, M)
     K = half // FB
     N = D * K
-    RS, RP = 4, D + 1
+    RS, RP = 4, D
     factor = 2.0 / math.sqrt(M * D)
-    cosine, sine = rope_tables(positions, cols, T, lax.axis_index("tensor"))
+    freq, rotates = rope_lanes(cols, T, lax.axis_index("tensor"))
     down = down_map.T
     down_wide = jnp.concatenate([jnp.zeros_like(down), down], axis=0)
     dma = pltpu.SemaphoreType.DMA
@@ -342,7 +383,7 @@
             jax.ShapeDtypeStruct((rank, F), f32),
             jax.ShapeDtypeStruct((rank, cols), f32),
         ),
-        in_specs=[vmem] * 7 + [pl.BlockSpec(memory_space=pl.ANY)],
+        in_specs=[vmem] * 8 + [pl.BlockSpec(memory_space=pl.ANY)],
         out_specs=(vmem, vmem, vmem),
         scratch_shapes=[
             pltpu.VMEM((M, cols), bf16),
@@ -351,6 +392,7 @@
             pltpu.VMEM((RS, M, FB), bf16),
             pltpu.VMEM((N + K, M, FB), bf16),
             pltpu.VMEM((RP, M, FB), f32),
+            pltpu.VMEM((K, M, FB), f32),
             pltpu.VMEM((T, 2 * rank, M // T), f32),
             pltpu.VMEM((T, 2 * rank, M // T), f32),
             pltpu.VMEM((T, 2 * rank, M // T), bf16),
@@ -376,7 +418,7 @@
         compiler_params=pltpu.CompilerParams(
             collective_id=0, has_side_effects=True, vmem_limit_bytes=63 * 1024 * 1024
         ),
-    )(g, cosine, sine, x, down, down_wide, up, w.reshape(2, half, cols))
+    )(g, positions[:, None], freq, rotates, x, down, down_wide, up, w.reshape(2, half, cols))
     return out, out_a.T, out_b
 
 

time: 232 us -> 224 us (0.966)
  other arithmetic: 7.89 us -> 1.17 us
  Pallas kernels: 217 us -> 214 us
    select_n x1 -> x0, other arithmetic: 7.16 us -> none  [rope_tables(): return (cosine, jnp.where(rotate, sine, jnp.float32(0.0)))]
    pallas_call x1, Pallas kernels: 217 us -> 214 us  [fused(): pl.pallas_call(functools.partial(fused_kernel, (D, K, FB, TB, RS, RP, fac...]
where the time goes in v3:
time: 224 us; the launch traced here: 223 us
  Pallas kernels  214 us (96%)
  local copies, waits for them, and re-layouts  7.49 us (3%)
    pallas_call x1, Pallas kernels, fused(): pl.pallas_call(functools.partial(fused_kernel, (D, K, FB, TB, RS, RP, fac...  214 us

profile of v3, /device:TPU:6, one launch (start us, length us, event | category | flops | bytes accessed | tf_op | source)
XLA Modules:
  0.0 222.9 jit_solution(1165744396257464468)
XLA Ops:
  0.6 0.6 multiply_power_fusion.freq
  1.2 0.6 compare_convert_fusion.rotates
  1.8 1.4 concatenate.3.down_wide
  3.2 1.7 copy.9.positions
  4.9 213.6 %shard_map.85 = (bf16[1024,1024]{1,0:T(8,128)(2,1)}, f32[16,1024]{1,0:T(8,128)}, f32[16,1280]{1,0:T(8,128)}) custom-call(bf16[1024,1280]{1,0:T(8,128)(2,1)} %g.1, s32[1024,1]{1,0:T(8,128)} %copy.9.positions, f32[1,384]{1,0:T(1,128)} %multiply_power_fusion.freq, f32[1,384]{1,0:T(1,128)} %compare_convert_fusion.rotates, bf16[1024,1024]{1,0:T(8,128)(2,1)} %x.3, ...), custom_call_target="tpu_custom_call" | custom-call | tf_op jit(solution)/shard_map/pallas_call | solution.py:379
  218.5 0.0 copy-start.1
  218.5 0.0 copy-start
  218.5 3.1 %copy.13 = bf16[1024,1024]{1,0:T(8,128)(2,1)} copy(bf16[1024,1024]{1,0:T(8,128)(2,1)} %get-tuple-element.12) | data formatting | bytes 4194304
  221.7 0.0 copy-done.1
  221.7 0.6 copy.14
  222.3 0.0 copy-done
  222.3 0.6 copy.15
Async XLA Ops:
  218.5 3.1 %copy-start.1 = (f32[16,1024]{1,0:T(8,128)S(1)}, f32[16,1024]{1,0:T(8,128)}, u32[]{:S(2)}) copy-start(f32[16,1024]{1,0:T(8,128)} %get-tuple-element.7) | copy-start | bytes 196612
  218.5 3.8 %copy-start = (f32[16,1280]{1,0:T(8,128)S(1)}, f32[16,1280]{1,0:T(8,128)}, u32[]{:S(2)}) copy-start(f32[16,1280]{1,0:T(8,128)} %get-tuple-element.14) | copy-start | bytes 245764

commit v4 on v3

--- a/solution.py
+++ b/solution.py
@@ -32,7 +32,7 @@
     load_sem, wsend_sem, wrecv_sem, relay_sem, psend_sem, prx_sem, zsend_sem, zrx_sem,
     low_s1, low_r1, low_s2, low_r2, ab_s, ab_r,
 ):
-    D, K, FB, TB, RS, RP, factor = sizes
+    D, K, FB, TB, S, RS, RP, factor = sizes
     Z = D
     T = 2 * D
     N = D * K
@@ -204,17 +204,21 @@
     def extra_slot(j):
         return N + place(j)[1]
 
-    def line_copy(j):
+    def part(q):
+        return pl.ds(pl.multiple_of(q * (M // S), M // S), M // S)
+
+    def line_copy(j, q):
         p = owner_at(place(j)[0])
         slot = jnp.where(p == z - 1, extra_slot(j), j)
         return pltpu.make_async_remote_copy(
-            src_ref=prx.at[j], dst_ref=zrx.at[slot],
-            send_sem=zsend_sem.at[j], recv_sem=zrx_sem.at[slot],
+            src_ref=prx.at[j, part(q), :], dst_ref=zrx.at[slot, part(q), :],
+            send_sem=zsend_sem.at[j, q], recv_sem=zrx_sem.at[slot, q],
             device_id={"tensor": t + jnp.where(p > z, 2, -2)}, device_id_type=MESH,
         )
 
-    def arrived(slot):
-        return pltpu.make_async_copy(zrx.at[slot], zrx.at[slot], zrx_sem.at[slot])
+    def arrived(slot, q):
+        block = zrx.at[slot, part(q), :]
+        return pltpu.make_async_copy(block, block, zrx_sem.at[slot, q])
 
     def produce(it):
         r, k = place(it)
@@ -249,43 +253,51 @@
         r, k = place(j)
         p = owner_at(r)
         partner_copy(j).wait_recv()
-        pend[j % RP] += prx[j].astype(jnp.float32)
-
-        @pl.when(jnp.logical_and(z < p, z > 0))
-        def _():
-            arrived(j).wait()
-            pend[j % RP] += zrx[j].astype(jnp.float32)
-
-        @pl.when(jnp.logical_and(z > p, z < Z - 1))
-        def _():
-            arrived(j).wait()
-            pend[j % RP] += zrx[j].astype(jnp.float32)
+        inner = jnp.logical_or(
+            jnp.logical_and(z < p, z > 0), jnp.logical_and(z > p, z < Z - 1)
+        )
 
         @pl.when(p == z)
         def _():
-            fin[k] = pend[j % RP]
+            fin[k] = pend[j % RP] + prx[j].astype(jnp.float32)
 
         @pl.when(p != z)
         def _():
-            prx[j] = pend[j % RP].astype(jnp.bfloat16)
-            line_copy(j).start()
+            @pl.loop(0, S)
+            def _(q):
+                rows = part(q)
+                pend[j % RP, rows, :] += prx[j, rows, :].astype(jnp.float32)
+
+                @pl.when(inner)
+                def _():
+                    arrived(j, q).wait()
+                    pend[j % RP, rows, :] += zrx[j, rows, :].astype(jnp.float32)
+
+                prx[j, rows, :] = pend[j % RP, rows, :].astype(jnp.bfloat16)
+                line_copy(j, q).start()
 
     def finish(j):
         k = place(j)[1]
         at = pl.ds(pl.multiple_of(k * FB, FB), FB)
 
-        @pl.when(z > 0)
-        def _():
-            arrived(j).wait()
-            fin[k] += zrx[j].astype(jnp.float32)
-
-        @pl.when(z < Z - 1)
-        def _():
-            arrived(N + k).wait()
-            fin[k] += zrx[N + k].astype(jnp.float32)
-
-        extra = jnp.dot(low_tall[...], down_wide[:, at], preferred_element_type=jnp.float32)
-        out[:, at] = (fin[k] + 2.0 * extra).astype(jnp.bfloat16)
+        @pl.loop(0, S)
+        def _(q):
+            rows = part(q)
+
+            @pl.when(z > 0)
+            def _():
+                arrived(j, q).wait()
+                fin[k, rows, :] += zrx[j, rows, :].astype(jnp.float32)
+
+            @pl.when(z < Z - 1)
+            def _():
+                arrived(N + k, q).wait()
+                fin[k, rows, :] += zrx[N + k, rows, :].astype(jnp.float32)
+
+            extra = jnp.dot(
+                low_tall[rows, :], down_wide[:, at], preferred_element_type=jnp.float32
+            )
+            out[rows, at] = (fin[k, rows, :] + 2.0 * extra).astype(jnp.bfloat16)
 
     def upstream(j):
         p = owner_at(place(j)[0])
@@ -355,7 +367,8 @@
     def _(j):
         @pl.when(owner_at(place(j)[0]) != z)
         def _():
-            line_copy(j).wait_send()
+            for q in range(S):
+                line_copy(j, q).wait_send()
 
 
 def fused(x, positions, w, down_map, up, g, D):
@@ -368,7 +381,7 @@
     TB = min(512, M)
     K = half // FB
     N = D * K
-    RS, RP = 4, D
+    S, RS, RP = 4, 4, D
     factor = 2.0 / math.sqrt(M * D)
     freq, rotates = rope_lanes(cols, T, lax.axis_index("tensor"))
     down = down_map.T
@@ -377,7 +390,7 @@
     vmem = pl.BlockSpec(memory_space=pltpu.VMEM)
     f32, bf16 = jnp.float32, jnp.bfloat16
     out, out_a, out_b = pl.pallas_call(
-        functools.partial(fused_kernel, (D, K, FB, TB, RS, RP, factor)),
+        functools.partial(fused_kernel, (D, K, FB, TB, S, RS, RP, factor)),
         out_shape=(
             jax.ShapeDtypeStruct((M, half), bf16),
             jax.ShapeDtypeStruct((rank, F), f32),
@@ -406,8 +419,8 @@
             dma((K,)),
             dma((RS,)),
             dma((N,)),
-            dma((N,)),
-            dma((N + K,)),
+            dma((N, S)),
+            dma((N + K, S)),
             dma((T,)),
             dma((T,)),
             dma((T,)),

time: 224 us -> 221 us (0.987)
  Pallas kernels: 214 us -> 211 us
    pallas_call x1, Pallas kernels: 214 us -> 211 us  [fused(): pl.pallas_call(functools.partial(fused_kernel, (D, K, FB, TB, S, RS, RP,...]
where the time goes in v4:
time: 221 us; the launch traced here: 220 us
  Pallas kernels  211 us (95%)
  local copies, waits for them, and re-layouts  7.49 us (3%)
    pallas_call x1, Pallas kernels, fused(): pl.pallas_call(functools.partial(fused_kernel, (D, K, FB, TB, S, RS, RP,...  211 us

profile of v4, /device:TPU:6, one launch (start us, length us, event | category | flops | bytes accessed | tf_op | source)
XLA Modules:
  0.0 220.3 jit_solution(4418256240337128185)
XLA Ops:
  0.6 0.6 multiply_power_fusion.freq
  1.2 0.6 compare_convert_fusion.rotates
  1.8 1.4 concatenate.3.down_wide
  3.2 1.7 copy.9.positions
  4.9 211.0 %shard_map.85 = (bf16[1024,1024]{1,0:T(8,128)(2,1)}, f32[16,1024]{1,0:T(8,128)}, f32[16,1280]{1,0:T(8,128)}) custom-call(bf16[1024,1280]{1,0:T(8,128)(2,1)} %g.1, s32[1024,1]{1,0:T(8,128)} %copy.9.positions, f32[1,384]{1,0:T(1,128)} %multiply_power_fusion.freq, f32[1,384]{1,0:T(1,128)} %compare_convert_fusion.rotates, bf16[1024,1024]{1,0:T(8,128)(2,1)} %x.3, ...), custom_call_target="tpu_custom_call" | custom-call | tf_op jit(solution)/shard_map/pallas_call | solution.py:392
  215.9 0.0 copy-start.1
  215.9 0.0 copy-start
  215.9 3.1 %copy.13 = bf16[1024,1024]{1,0:T(8,128)(2,1)} copy(bf16[1024,1024]{1,0:T(8,128)(2,1)} %get-tuple-element.12) | data formatting | bytes 4194304
  219.1 0.0 copy-done.1
  219.1 0.6 copy.14
  219.7 0.0 copy-done
  219.7 0.6 copy.15
Async XLA Ops:
  215.9 3.1 %copy-start.1 = (f32[16,1024]{1,0:T(8,128)S(1)}, f32[16,1024]{1,0:T(8,128)}, u32[]{:S(2)}) copy-start(f32[16,1024]{1,0:T(8,128)} %get-tuple-element.7) | copy-start | bytes 196612
  215.9 3.8 %copy-start = (f32[16,1280]{1,0:T(8,128)S(1)}, f32[16,1280]{1,0:T(8,128)}, u32[]{:S(2)}) copy-start(f32[16,1280]{1,0:T(8,128)} %get-tuple-element.14) | copy-start | bytes 245764
